TPU v7x, 32 devices: a whole 2x2x4 slice. The times are simulated.
32 devices in a mesh: gz: 8 (over z, y), gy: 4 (over x, core).
Axes of the slice: x: 2, y: 2, z: 4, core: 2. Of those that a mesh axis runs over, the one named last changes fastest.
Arguments:
- block: float32 [8, 64, 128, 256], P(None, 'gz', 'gy'), may hold values from -6 to 6
- conduct: float32 [64, 128, 256], P('gz', 'gy'), may hold values from 0.5 to 2
Outputs:
- basis: float32 [8, 64, 128, 256], P(None, 'gz', 'gy')
All inputs are finite; a program needn't handle non-finite values.
Results may differ from a plain program's by a relative error of at most 0.00021.
Values sent between devices are 32-bit elements; how exact they have to be, the bound alone decides.
A program may use at most 128 MiB of HBM per device.

v0:
```python
import math

import jax
import jax.numpy as jnp
from jax import lax
from jax.sharding import PartitionSpec as P

DEG = 4


mid_point = 12.75
half_width = 11.25


def with_halo(block, sides, width):
    for axis, dim in sides:
        count = lax.axis_size(axis)
        forward = [(i, i + 1) for i in range(count - 1)]
        backward = [(target, source) for source, target in forward]
        low = lax.ppermute(
            lax.slice_in_dim(block, block.shape[dim] - width, None, axis=dim), axis, forward
        )
        high = lax.ppermute(lax.slice_in_dim(block, 0, width, axis=dim), axis, backward)
        block = jnp.concatenate([low, block, high], axis=dim)
    return block


def stencil(padded, kpadded):
    inner = slice(1, -1)
    centre = padded[:, 1:-1, 1:-1, 1:-1]
    kcentre = kpadded[1:-1, 1:-1, 1:-1]
    shifts = [
        (slice(2, None), inner, inner),
        (slice(None, -2), inner, inner),
        (inner, slice(2, None), inner),
        (inner, slice(None, -2), inner),
        (inner, inner, slice(2, None)),
        (inner, inner, slice(None, -2)),
    ]
    total = jnp.zeros_like(centre)
    for where in shifts:
        total = total + 0.5 * (kcentre + kpadded[where]) * (centre - padded[(slice(None),) + where])
    return total


def widen_field(array):
    return jnp.pad(array, ((0, 0), (0, 0), (0, 0), (1, 1)))


def widen_coef(array):
    return jnp.pad(array, ((0, 0), (0, 0), (1, 1)))


def single_step(current, previous, kpadded):
    padded = with_halo(current, (("gz", 1), ("gy", 2)), 1)
    image = stencil(widen_field(padded), widen_coef(kpadded))
    if previous is None:
        return (image - mid_point * current) / half_width
    return 2.0 * (image - mid_point * current) / half_width - previous


def shards(block, conduct):
    vectors, zcount, ycount, xcount = block.shape
    width, corners = (1, False)
    kpadded = with_halo(conduct, (("gz", 0), ("gy", 1)), width)
    field = block
    for passes in range(2):
        previous = None
        current = field
        for step in range(DEG):
            nextone = single_step(current, previous, kpadded)
            previous = current
            current = nextone
        field = current
    flat = field.reshape(vectors, -1)
    local_gram = jnp.dot(flat, flat.T, precision=lax.Precision.HIGHEST)
    gram = lax.psum(lax.psum(local_gram, "gy"), "gz")
    lower = jnp.linalg.cholesky(gram)
    inverse = lax.linalg.triangular_solve(
        lower, jnp.eye(vectors, dtype=jnp.float32), left_side=True, lower=True
    )
    total_cells = xcount * ycount * zcount * lax.axis_size("gz") * lax.axis_size("gy")
    scaled = jnp.dot(inverse, flat, precision=lax.Precision.HIGHEST) * math.sqrt(total_cells)
    return scaled.reshape(field.shape)


def solution(mesh):
    in_specs = (P(None, "gz", "gy", None), P("gz", "gy", None))
    out_specs = P(None, "gz", "gy", None)
    return jax.shard_map(shards, mesh=mesh, in_specs=in_specs, out_specs=out_specs, check_vma=False)
```

profile of v0, /device:TPU:0, one launch (start us, length us, event | category | flops | bytes accessed | tf_op | source)
XLA Modules:
  0.0 284.9 jit_solution(17703938605711166255)
XLA Ops:
  2.1 5.7 %collective-permute-start.2 = (f32[1,32,256]{2,1,0:T(8,128)S(1)}, f32[1,32,256]{2,1,0:T(8,128)S(1)}, u32[]{:S(2)}, u32[]{:S(2)}) collective-permute-start(f32[1,32,256]{2,1,0:T(8,128)S(1)} %get-tuple-element.53), channel_id=1, source_target_pairs={{0,4},{4,8},{8,12},{12,16},{16,20},{20,24},{24,28},{1,5},{5,9},{9,... | collective-permute-start | bytes 98312 | tf_op jit(solution)/shard_map/ppermute | solution.py:20
  10.6 5.0 %collective-permute-start.3 = (f32[8,1,32,256]{3,0,2,1:T(8,128)S(1)}, f32[8,1,32,256]{3,0,2,1:T(8,128)S(1)}, u32[]{:S(2)}, u32[]{:S(2)}) collective-permute-start(f32[8,1,32,256]{3,0,2,1:T(8,128)S(1)} %get-tuple-element.40), channel_id=1, source_target_pairs={{0,4},{4,8},{8,12},{12,16},{16,20},{20,24},{24,28},{1,5},{5,9},{9,... | collective-permute-start | bytes 786440 | tf_op jit(solution)/shard_map/ppermute | solution.py:20
  23.4 4.1 %collective-permute-done.1 = f32[8,1,32,256]{3,0,2,1:T(8,128)S(1)} collective-permute-done((f32[8,1,32,256]{3,0,2,1:T(8,128)S(1)}, f32[8,1,32,256]{3,0,2,1:T(8,128)S(1)}, u32[]{:S(2)}, u32[]{:S(2)}) %collective-permute-start.1) | collective-permute-done | bytes 262176 | tf_op jit(solution)/shard_map/ppermute | solution.py:23
  48.7 4.7 %collective-permute-done.8 = f32[8,1,32,256]{3,0,2,1:T(8,128)S(1)} collective-permute-done((f32[8,1,32,256]{3,0,2,1:T(8,128)S(1)}, f32[8,1,32,256]{3,0,2,1:T(8,128)S(1)}, u32[]{:S(2)}, u32[]{:S(2)}) %collective-permute-start.8) | collective-permute-done | bytes 262176 | tf_op jit(solution)/shard_map/ppermute | solution.py:23
  53.4 5.1 %collective-permute-start.11 = (f32[8,10,1,256]{3,0,2,1:T(8,128)S(1)}, f32[8,10,1,256]{3,0,2,1:T(8,128)S(1)}, u32[]{:S(2)}, u32[]{:S(2)}) collective-permute-start(f32[8,10,1,256]{3,0,2,1:T(8,128)S(1)} %get-tuple-element.21), channel_id=1, source_target_pairs={{0,1},{1,2},{2,3},{4,5},{5,6},{6,7},{8,9},{9,10},{10,11},{12,13},{... | collective-permute-start | bytes 245768 | tf_op jit(solution)/shard_map/ppermute | solution.py:20
  64.7 5.5 %fusion.111 = f32[8,8,32,256]{3,0,2,1:T(8,128)S(1)} fusion(f32[8,8,32,256]{3,0,2,1:T(8,128)S(1)} %get-tuple-element.7, f32[8,10,34,258]{3,0,2,1:T(8,128)S(1)} %select_maximum_fusion.24, f32[8,10,1,256]{3,0,2,1:T(8,128)S(1)} %collective-permute-done.11, f32[8,1,32,256]{3,0,2,1:T(8,128)S(1)} %collective-permute-done.8, ...), kind=kLoop, calls=%fused_computation.205 | loop fusion | flops 15204352 | bytes 14843904 | tf_op jit(solution)/shard_map/sub | solution.py:59
  70.3 4.1 %collective-permute-start.13 = (f32[8,1,32,256]{3,0,2,1:T(8,128)S(1)}, f32[8,1,32,256]{3,0,2,1:T(8,128)S(1)}, u32[]{:S(2)}, u32[]{:S(2)}) collective-permute-start(f32[8,1,32,256]{3,0,2,1:T(8,128)S(1)} %get-tuple-element.35), channel_id=1, source_target_pairs={{0,4},{4,8},{8,12},{12,16},{16,20},{20,24},{24,28},{1,5},{5,9},{9,... | collective-permute-start | bytes 786440 | tf_op jit(solution)/shard_map/ppermute | solution.py:20
  79.0 5.4 %collective-permute-done.12 = f32[8,1,32,256]{3,0,2,1:T(8,128)S(1)} collective-permute-done((f32[8,1,32,256]{3,0,2,1:T(8,128)S(1)}, f32[8,1,32,256]{3,0,2,1:T(8,128)S(1)}, u32[]{:S(2)}, u32[]{:S(2)}) %collective-permute-start.12) | collective-permute-done | bytes 262176 | tf_op jit(solution)/shard_map/ppermute | solution.py:23
  97.9 4.6 %collective-permute-start.17 = (f32[8,1,32,256]{3,0,2,1:T(8,128)S(1)}, f32[8,1,32,256]{3,0,2,1:T(8,128)S(1)}, u32[]{:S(2)}, u32[]{:S(2)}) collective-permute-start(f32[8,1,32,256]{3,0,2,1:T(8,128)S(1)} %get-tuple-element.33), channel_id=1, source_target_pairs={{0,4},{4,8},{8,12},{12,16},{16,20},{20,24},{24,28},{1,5},{5,9},{9,... | collective-permute-start | bytes 786440 | tf_op jit(solution)/shard_map/ppermute | solution.py:20
  107.2 6.4 %collective-permute-done.16 = f32[8,1,32,256]{3,0,2,1:T(8,128)S(1)} collective-permute-done((f32[8,1,32,256]{3,0,2,1:T(8,128)S(1)}, f32[8,1,32,256]{3,0,2,1:T(8,128)S(1)}, u32[]{:S(2)}, u32[]{:S(2)}) %collective-permute-start.16) | collective-permute-done | bytes 262176 | tf_op jit(solution)/shard_map/ppermute | solution.py:23
  126.6 4.8 %collective-permute-start.21 = (f32[8,1,32,256]{3,0,2,1:T(8,128)S(1)}, f32[8,1,32,256]{3,0,2,1:T(8,128)S(1)}, u32[]{:S(2)}, u32[]{:S(2)}) collective-permute-start(f32[8,1,32,256]{3,0,2,1:T(8,128)S(1)} %get-tuple-element.31), channel_id=1, source_target_pairs={{0,4},{4,8},{8,12},{12,16},{16,20},{20,24},{24,28},{1,5},{5,9},{9,... | collective-permute-start | bytes 786440 | tf_op jit(solution)/shard_map/ppermute | solution.py:20
  132.7 3.7 %collective-permute-done.21 = f32[8,1,32,256]{3,0,2,1:T(8,128)S(1)} collective-permute-done((f32[8,1,32,256]{3,0,2,1:T(8,128)S(1)}, f32[8,1,32,256]{3,0,2,1:T(8,128)S(1)}, u32[]{:S(2)}, u32[]{:S(2)}) %collective-permute-start.21) | collective-permute-done | bytes 262176 | tf_op jit(solution)/shard_map/ppermute | solution.py:20
  136.4 6.3 %collective-permute-done.20 = f32[8,1,32,256]{3,0,2,1:T(8,128)S(1)} collective-permute-done((f32[8,1,32,256]{3,0,2,1:T(8,128)S(1)}, f32[8,1,32,256]{3,0,2,1:T(8,128)S(1)}, u32[]{:S(2)}, u32[]{:S(2)}) %collective-permute-start.20) | collective-permute-done | bytes 262176 | tf_op jit(solution)/shard_map/ppermute | solution.py:23
  155.5 4.8 %collective-permute-start.25 = (f32[8,1,32,256]{3,0,2,1:T(8,128)S(1)}, f32[8,1,32,256]{3,0,2,1:T(8,128)S(1)}, u32[]{:S(2)}, u32[]{:S(2)}) collective-permute-start(f32[8,1,32,256]{3,0,2,1:T(8,128)S(1)} %get-tuple-element.29), channel_id=1, source_target_pairs={{0,4},{4,8},{8,12},{12,16},{16,20},{20,24},{24,28},{1,5},{5,9},{9,... | collective-permute-start | bytes 786440 | tf_op jit(solution)/shard_map/ppermute | solution.py:20
  161.7 3.7 %collective-permute-done.25 = f32[8,1,32,256]{3,0,2,1:T(8,128)S(1)} collective-permute-done((f32[8,1,32,256]{3,0,2,1:T(8,128)S(1)}, f32[8,1,32,256]{3,0,2,1:T(8,128)S(1)}, u32[]{:S(2)}, u32[]{:S(2)}) %collective-permute-start.25) | collective-permute-done | bytes 262176 | tf_op jit(solution)/shard_map/ppermute | solution.py:20
  165.4 6.3 %collective-permute-done.24 = f32[8,1,32,256]{3,0,2,1:T(8,128)S(1)} collective-permute-done((f32[8,1,32,256]{3,0,2,1:T(8,128)S(1)}, f32[8,1,32,256]{3,0,2,1:T(8,128)S(1)}, u32[]{:S(2)}, u32[]{:S(2)}) %collective-permute-start.24) | collective-permute-done | bytes 262176 | tf_op jit(solution)/shard_map/ppermute | solution.py:23
  184.9 4.8 %collective-permute-start.29 = (f32[8,1,32,256]{3,0,2,1:T(8,128)S(1)}, f32[8,1,32,256]{3,0,2,1:T(8,128)S(1)}, u32[]{:S(2)}, u32[]{:S(2)}) collective-permute-start(f32[8,1,32,256]{3,0,2,1:T(8,128)S(1)} %get-tuple-element.27), channel_id=1, source_target_pairs={{0,4},{4,8},{8,12},{12,16},{16,20},{20,24},{24,28},{1,5},{5,9},{9,... | collective-permute-start | bytes 786440 | tf_op jit(solution)/shard_map/ppermute | solution.py:20
  191.0 3.7 %collective-permute-done.29 = f32[8,1,32,256]{3,0,2,1:T(8,128)S(1)} collective-permute-done((f32[8,1,32,256]{3,0,2,1:T(8,128)S(1)}, f32[8,1,32,256]{3,0,2,1:T(8,128)S(1)}, u32[]{:S(2)}, u32[]{:S(2)}) %collective-permute-start.29) | collective-permute-done | bytes 262176 | tf_op jit(solution)/shard_map/ppermute | solution.py:20
  194.7 6.3 %collective-permute-done.28 = f32[8,1,32,256]{3,0,2,1:T(8,128)S(1)} collective-permute-done((f32[8,1,32,256]{3,0,2,1:T(8,128)S(1)}, f32[8,1,32,256]{3,0,2,1:T(8,128)S(1)}, u32[]{:S(2)}, u32[]{:S(2)}) %collective-permute-start.28) | collective-permute-done | bytes 262176 | tf_op jit(solution)/shard_map/ppermute | solution.py:23
  214.1 4.8 %collective-permute-start.33 = (f32[8,1,32,256]{3,0,2,1:T(8,128)S(1)}, f32[8,1,32,256]{3,0,2,1:T(8,128)S(1)}, u32[]{:S(2)}, u32[]{:S(2)}) collective-permute-start(f32[8,1,32,256]{3,0,2,1:T(8,128)S(1)} %get-tuple-element.25), channel_id=1, source_target_pairs={{0,4},{4,8},{8,12},{12,16},{16,20},{20,24},{24,28},{1,5},{5,9},{9,... | collective-permute-start | bytes 786440 | tf_op jit(solution)/shard_map/ppermute | solution.py:20
  223.9 6.3 %collective-permute-done.32 = f32[8,1,32,256]{3,0,2,1:T(8,128)S(1)} collective-permute-done((f32[8,1,32,256]{3,0,2,1:T(8,128)S(1)}, f32[8,1,32,256]{3,0,2,1:T(8,128)S(1)}, u32[]{:S(2)}, u32[]{:S(2)}) %collective-permute-start.32) | collective-permute-done | bytes 262176 | tf_op jit(solution)/shard_map/ppermute | solution.py:23
  243.2 4.6 %convolution_bitcast_fusion = f32[8,8]{0,1:T(8,128)S(1)} fusion(f32[8,8,32,256]{3,0,2,1:T(8,128)S(1)} %fusion.5), kind=kOutput, calls=%fused_computation.250 | convolution fusion | flops 50331648 | bytes 2097408 | tf_op jit(solution)/shard_map/dot_general | solution.py:76
  247.7 8.2 %psum.14 = f32[8,8]{0,1:T(8,128)S(1)} all-reduce(f32[8,8]{0,1:T(8,128)S(1)} %convolution_bitcast_fusion), channel_id=1, replica_groups=mesh['gz'=8,'gy'=4] {'gy'}, use_global_device_ids=true, to_apply=%region_0.1 | all-reduce | flops 64 | bytes 512 | tf_op jit(solution)/shard_map/psum | solution.py:77
  256.0 22.2 %psum.15 = f32[8,8]{0,1:T(8,128)S(1)} all-reduce(f32[8,8]{0,1:T(8,128)S(1)} %psum.14), channel_id=1, replica_groups=mesh['gz'=8,'gy'=4] {'gz'}, use_global_device_ids=true, to_apply=%region_1.2 | all-reduce | flops 64 | bytes 512 | tf_op jit(solution)/shard_map/psum | solution.py:77
  (108 shorter events, 143.1 us)
Async XLA Ops:
  0.8 14.8 %collective-permute-start = (f32[1,32,256]{2,1,0:T(8,128)S(1)}, f32[1,32,256]{2,1,0:T(8,128)S(1)}, u32[]{:S(2)}, u32[]{:S(2)}) collective-permute-start(f32[1,32,256]{2,1,0:T(8,128)S(1)} %get-tuple-element.52), channel_id=1, source_target_pairs={{4,0},{8,4},{12,8},{16,12},{20,16},{24,20},{28,24},{5,1},{9,5},{13... | collective-permute-start | bytes 98312 | tf_op jit(solution)/shard_map/ppermute | solution.py:23
  2.1 13.5 %collective-permute-start.2 = (f32[1,32,256]{2,1,0:T(8,128)S(1)}, f32[1,32,256]{2,1,0:T(8,128)S(1)}, u32[]{:S(2)}, u32[]{:S(2)}) collective-permute-start(f32[1,32,256]{2,1,0:T(8,128)S(1)} %get-tuple-element.53), channel_id=1, source_target_pairs={{0,4},{4,8},{8,12},{12,16},{16,20},{20,24},{24,28},{1,5},{5,9},{9,... | collective-permute-start | bytes 98312 | tf_op jit(solution)/shard_map/ppermute | solution.py:20
  10.6 11.5 %collective-permute-start.3 = (f32[8,1,32,256]{3,0,2,1:T(8,128)S(1)}, f32[8,1,32,256]{3,0,2,1:T(8,128)S(1)}, u32[]{:S(2)}, u32[]{:S(2)}) collective-permute-start(f32[8,1,32,256]{3,0,2,1:T(8,128)S(1)} %get-tuple-element.40), channel_id=1, source_target_pairs={{0,4},{4,8},{8,12},{12,16},{16,20},{20,24},{24,28},{1,5},{5,9},{9,... | collective-permute-start | bytes 786440 | tf_op jit(solution)/shard_map/ppermute | solution.py:20
  17.0 4.8 %collective-permute-start.4 = (f32[10,1,256]{2,1,0:T(1,128)S(1)}, f32[10,1,256]{2,1,0:T(1,128)S(1)}, u32[]{:S(2)}, u32[]{:S(2)}) collective-permute-start(f32[10,1,256]{2,1,0:T(1,128)S(1)} %get-tuple-element.46), channel_id=1, source_target_pairs={{1,0},{2,1},{3,2},{5,4},{6,5},{7,6},{9,8},{10,9},{11,10},{13,12},{... | collective-permute-start | bytes 30728 | tf_op jit(solution)/shard_map/ppermute | solution.py:23
  18.3 9.2 %collective-permute-start.1 = (f32[8,1,32,256]{3,0,2,1:T(8,128)S(1)}, f32[8,1,32,256]{3,0,2,1:T(8,128)S(1)}, u32[]{:S(2)}, u32[]{:S(2)}) collective-permute-start(f32[8,1,32,256]{3,0,2,1:T(8,128)S(1)} %get-tuple-element.39), channel_id=1, source_target_pairs={{4,0},{8,4},{12,8},{16,12},{20,16},{24,20},{28,24},{5,1},{9,5},{13... | collective-permute-start | bytes 786440 | tf_op jit(solution)/shard_map/ppermute | solution.py:23
  27.6 5.1 %collective-permute-start.7 = (f32[8,10,1,256]{3,0,2,1:T(8,128)S(1)}, f32[8,10,1,256]{3,0,2,1:T(8,128)S(1)}, u32[]{:S(2)}, u32[]{:S(2)}) collective-permute-start(f32[8,10,1,256]{3,0,2,1:T(8,128)S(1)} %get-tuple-element.23), channel_id=1, source_target_pairs={{0,1},{1,2},{2,3},{4,5},{5,6},{6,7},{8,9},{9,10},{10,11},{12,13},{... | collective-permute-start | bytes 245768 | tf_op jit(solution)/shard_map/ppermute | solution.py:20
  31.2 5.2 %collective-permute-start.5 = (f32[8,10,1,256]{3,0,2,1:T(8,128)S(1)}, f32[8,10,1,256]{3,0,2,1:T(8,128)S(1)}, u32[]{:S(2)}, u32[]{:S(2)}) collective-permute-start(f32[8,10,1,256]{3,0,2,1:T(8,128)S(1)} %get-tuple-element.24), channel_id=1, source_target_pairs={{1,0},{2,1},{3,2},{5,4},{6,5},{7,6},{9,8},{10,9},{11,10},{13,12},{... | collective-permute-start | bytes 245768 | tf_op jit(solution)/shard_map/ppermute | solution.py:23
  40.7 8.0 %collective-permute-start.9 = (f32[8,1,32,256]{3,0,2,1:T(8,128)S(1)}, f32[8,1,32,256]{3,0,2,1:T(8,128)S(1)}, u32[]{:S(2)}, u32[]{:S(2)}) collective-permute-start(f32[8,1,32,256]{3,0,2,1:T(8,128)S(1)} %get-tuple-element.37), channel_id=1, source_target_pairs={{0,4},{4,8},{8,12},{12,16},{16,20},{20,24},{24,28},{1,5},{5,9},{9,... | collective-permute-start | bytes 786440 | tf_op jit(solution)/shard_map/ppermute | solution.py:20
  44.2 9.2 %collective-permute-start.8 = (f32[8,1,32,256]{3,0,2,1:T(8,128)S(1)}, f32[8,1,32,256]{3,0,2,1:T(8,128)S(1)}, u32[]{:S(2)}, u32[]{:S(2)}) collective-permute-start(f32[8,1,32,256]{3,0,2,1:T(8,128)S(1)} %get-tuple-element.38), channel_id=1, source_target_pairs={{4,0},{8,4},{12,8},{16,12},{20,16},{24,20},{28,24},{5,1},{9,5},{13... | collective-permute-start | bytes 786440 | tf_op jit(solution)/shard_map/ppermute | solution.py:23
  53.4 6.4 %collective-permute-start.11 = (f32[8,10,1,256]{3,0,2,1:T(8,128)S(1)}, f32[8,10,1,256]{3,0,2,1:T(8,128)S(1)}, u32[]{:S(2)}, u32[]{:S(2)}) collective-permute-start(f32[8,10,1,256]{3,0,2,1:T(8,128)S(1)} %get-tuple-element.21), channel_id=1, source_target_pairs={{0,1},{1,2},{2,3},{4,5},{5,6},{6,7},{8,9},{9,10},{10,11},{12,13},{... | collective-permute-start | bytes 245768 | tf_op jit(solution)/shard_map/ppermute | solution.py:20
  70.3 8.8 %collective-permute-start.13 = (f32[8,1,32,256]{3,0,2,1:T(8,128)S(1)}, f32[8,1,32,256]{3,0,2,1:T(8,128)S(1)}, u32[]{:S(2)}, u32[]{:S(2)}) collective-permute-start(f32[8,1,32,256]{3,0,2,1:T(8,128)S(1)} %get-tuple-element.35), channel_id=1, source_target_pairs={{0,4},{4,8},{8,12},{12,16},{16,20},{20,24},{24,28},{1,5},{5,9},{9,... | collective-permute-start | bytes 786440 | tf_op jit(solution)/shard_map/ppermute | solution.py:20
  74.4 10.0 %collective-permute-start.12 = (f32[8,1,32,256]{3,0,2,1:T(8,128)S(1)}, f32[8,1,32,256]{3,0,2,1:T(8,128)S(1)}, u32[]{:S(2)}, u32[]{:S(2)}) collective-permute-start(f32[8,1,32,256]{3,0,2,1:T(8,128)S(1)} %get-tuple-element.36), channel_id=1, source_target_pairs={{4,0},{8,4},{12,8},{16,12},{20,16},{24,20},{28,24},{5,1},{9,5},{13... | collective-permute-start | bytes 786440 | tf_op jit(solution)/shard_map/ppermute | solution.py:23
  97.9 9.3 %collective-permute-start.17 = (f32[8,1,32,256]{3,0,2,1:T(8,128)S(1)}, f32[8,1,32,256]{3,0,2,1:T(8,128)S(1)}, u32[]{:S(2)}, u32[]{:S(2)}) collective-permute-start(f32[8,1,32,256]{3,0,2,1:T(8,128)S(1)} %get-tuple-element.33), channel_id=1, source_target_pairs={{0,4},{4,8},{8,12},{12,16},{16,20},{20,24},{24,28},{1,5},{5,9},{9,... | collective-permute-start | bytes 786440 | tf_op jit(solution)/shard_map/ppermute | solution.py:20
  102.5 11.1 %collective-permute-start.16 = (f32[8,1,32,256]{3,0,2,1:T(8,128)S(1)}, f32[8,1,32,256]{3,0,2,1:T(8,128)S(1)}, u32[]{:S(2)}, u32[]{:S(2)}) collective-permute-start(f32[8,1,32,256]{3,0,2,1:T(8,128)S(1)} %get-tuple-element.34), channel_id=1, source_target_pairs={{4,0},{8,4},{12,8},{16,12},{20,16},{24,20},{28,24},{5,1},{9,5},{13... | collective-permute-start | bytes 786440 | tf_op jit(solution)/shard_map/ppermute | solution.py:23
  113.6 4.9 %collective-permute-start.19 = (f32[8,10,1,256]{3,0,2,1:T(8,128)S(1)}, f32[8,10,1,256]{3,0,2,1:T(8,128)S(1)}, u32[]{:S(2)}, u32[]{:S(2)}) collective-permute-start(f32[8,10,1,256]{3,0,2,1:T(8,128)S(1)} %get-tuple-element.17), channel_id=1, source_target_pairs={{0,1},{1,2},{2,3},{4,5},{5,6},{6,7},{8,9},{9,10},{10,11},{12,13},{... | collective-permute-start | bytes 245768 | tf_op jit(solution)/shard_map/ppermute | solution.py:20
  126.6 9.9 %collective-permute-start.21 = (f32[8,1,32,256]{3,0,2,1:T(8,128)S(1)}, f32[8,1,32,256]{3,0,2,1:T(8,128)S(1)}, u32[]{:S(2)}, u32[]{:S(2)}) collective-permute-start(f32[8,1,32,256]{3,0,2,1:T(8,128)S(1)} %get-tuple-element.31), channel_id=1, source_target_pairs={{0,4},{4,8},{8,12},{12,16},{16,20},{20,24},{24,28},{1,5},{5,9},{9,... | collective-permute-start | bytes 786440 | tf_op jit(solution)/shard_map/ppermute | solution.py:20
  131.4 11.3 %collective-permute-start.20 = (f32[8,1,32,256]{3,0,2,1:T(8,128)S(1)}, f32[8,1,32,256]{3,0,2,1:T(8,128)S(1)}, u32[]{:S(2)}, u32[]{:S(2)}) collective-permute-start(f32[8,1,32,256]{3,0,2,1:T(8,128)S(1)} %get-tuple-element.32), channel_id=1, source_target_pairs={{4,0},{8,4},{12,8},{16,12},{20,16},{24,20},{28,24},{5,1},{9,5},{13... | collective-permute-start | bytes 786440 | tf_op jit(solution)/shard_map/ppermute | solution.py:23
  155.5 9.9 %collective-permute-start.25 = (f32[8,1,32,256]{3,0,2,1:T(8,128)S(1)}, f32[8,1,32,256]{3,0,2,1:T(8,128)S(1)}, u32[]{:S(2)}, u32[]{:S(2)}) collective-permute-start(f32[8,1,32,256]{3,0,2,1:T(8,128)S(1)} %get-tuple-element.29), channel_id=1, source_target_pairs={{0,4},{4,8},{8,12},{12,16},{16,20},{20,24},{24,28},{1,5},{5,9},{9,... | collective-permute-start | bytes 786440 | tf_op jit(solution)/shard_map/ppermute | solution.py:20
  160.4 11.3 %collective-permute-start.24 = (f32[8,1,32,256]{3,0,2,1:T(8,128)S(1)}, f32[8,1,32,256]{3,0,2,1:T(8,128)S(1)}, u32[]{:S(2)}, u32[]{:S(2)}) collective-permute-start(f32[8,1,32,256]{3,0,2,1:T(8,128)S(1)} %get-tuple-element.30), channel_id=1, source_target_pairs={{4,0},{8,4},{12,8},{16,12},{20,16},{24,20},{28,24},{5,1},{9,5},{13... | collective-permute-start | bytes 786440 | tf_op jit(solution)/shard_map/ppermute | solution.py:23
  184.9 9.9 %collective-permute-start.29 = (f32[8,1,32,256]{3,0,2,1:T(8,128)S(1)}, f32[8,1,32,256]{3,0,2,1:T(8,128)S(1)}, u32[]{:S(2)}, u32[]{:S(2)}) collective-permute-start(f32[8,1,32,256]{3,0,2,1:T(8,128)S(1)} %get-tuple-element.27), channel_id=1, source_target_pairs={{0,4},{4,8},{8,12},{12,16},{16,20},{20,24},{24,28},{1,5},{5,9},{9,... | collective-permute-start | bytes 786440 | tf_op jit(solution)/shard_map/ppermute | solution.py:20
  189.7 11.3 %collective-permute-start.28 = (f32[8,1,32,256]{3,0,2,1:T(8,128)S(1)}, f32[8,1,32,256]{3,0,2,1:T(8,128)S(1)}, u32[]{:S(2)}, u32[]{:S(2)}) collective-permute-start(f32[8,1,32,256]{3,0,2,1:T(8,128)S(1)} %get-tuple-element.28), channel_id=1, source_target_pairs={{4,0},{8,4},{12,8},{16,12},{20,16},{24,20},{28,24},{5,1},{9,5},{13... | collective-permute-start | bytes 786440 | tf_op jit(solution)/shard_map/ppermute | solution.py:23
  214.1 9.9 %collective-permute-start.33 = (f32[8,1,32,256]{3,0,2,1:T(8,128)S(1)}, f32[8,1,32,256]{3,0,2,1:T(8,128)S(1)}, u32[]{:S(2)}, u32[]{:S(2)}) collective-permute-start(f32[8,1,32,256]{3,0,2,1:T(8,128)S(1)} %get-tuple-element.25), channel_id=1, source_target_pairs={{0,4},{4,8},{8,12},{12,16},{16,20},{20,24},{24,28},{1,5},{5,9},{9,... | collective-permute-start | bytes 786440 | tf_op jit(solution)/shard_map/ppermute | solution.py:20
  218.9 11.3 %collective-permute-start.32 = (f32[8,1,32,256]{3,0,2,1:T(8,128)S(1)}, f32[8,1,32,256]{3,0,2,1:T(8,128)S(1)}, u32[]{:S(2)}, u32[]{:S(2)}) collective-permute-start(f32[8,1,32,256]{3,0,2,1:T(8,128)S(1)} %get-tuple-element.26), channel_id=1, source_target_pairs={{4,0},{8,4},{12,8},{16,12},{20,16},{24,20},{28,24},{5,1},{9,5},{13... | collective-permute-start | bytes 786440 | tf_op jit(solution)/shard_map/ppermute | solution.py:23
  230.2 4.9 %collective-permute-start.35 = (f32[8,10,1,256]{3,0,2,1:T(8,128)S(1)}, f32[8,10,1,256]{3,0,2,1:T(8,128)S(1)}, u32[]{:S(2)}, u32[]{:S(2)}) collective-permute-start(f32[8,10,1,256]{3,0,2,1:T(8,128)S(1)} %get-tuple-element.9), channel_id=1, source_target_pairs={{0,1},{1,2},{2,3},{4,5},{5,6},{6,7},{8,9},{9,10},{10,11},{12,13},{... | collective-permute-start | bytes 245768 | tf_op jit(solution)/shard_map/ppermute | solution.py:20
  (14 other events, 70.4 us)
where the time goes:
time: 286 us; the launch traced here: 285 us
  starting transfers between devices  95.9 us (34%)
  waiting for transfers between devices  89.7 us (31%)
  other arithmetic  54.4 us (19%)
  blocking collectives  30.4 us (11%)
  local copies, waits for them, and re-layouts  7.18 us (3%)
  matrix products  6.63 us (2%)
    ppermute x18, starting transfers between devices, with_halo(): lax.ppermute(lax.slice_in_dim(block, block.shape[dim] - width, None, axis...  72.2 us
    ppermute x18, waiting for transfers between devices, with_halo(): lax.ppermute(lax.slice_in_dim(block, 0, width, axis=dim), axis, backward)  64.7 us
    psum x2, blocking collectives, shards(): gram = lax.psum(lax.psum(local_gram, 'gy'), 'gz')  30.4 us
    ppermute x18, waiting for transfers between devices, with_halo(): lax.ppermute(lax.slice_in_dim(block, block.shape[dim] - width, None, axis...  25 us
    ppermute x18, starting transfers between devices, with_halo(): lax.ppermute(lax.slice_in_dim(block, 0, width, axis=dim), axis, backward)  23.6 us
    sub x6, other arithmetic, single_step(): return 2.0 * (image - mid_point * current) / half_width - previous  22.7 us
    concatenate x16, other arithmetic, with_halo(): block = jnp.concatenate([low, block, high], axis=dim)  22.5 us
    div x2, other arithmetic, single_step(): return (image - mid_point * current) / half_width  6.3 us
  transfers between devices with their start and end apart: 36, of which 24 were waited for; matrix products, arithmetic and copies ran while one was open for 2% of the time, Pallas kernels for 0%

commit v1 on v0

v1 whole, which is shorter than its diff:
```python
import functools
import math

import jax
import jax.numpy as jnp
from jax import lax
from jax.experimental import pallas as pl
from jax.experimental.pallas import tpu as pltpu
from jax.sharding import PartitionSpec as P

DEG = 4
PASSES = 2
STEPS = DEG * PASSES
STRIDE = 2

mid_point = 12.75
half_width = 11.25


def kernel(
    nz, ny,
    block, conduct, filtered, gram_out,
    field, coef, wz, wym, wyp, wxm, wxp, diag,
    yhalo, ysend, gathered, pairs, gsum_y, gsum_z,
    zs, zr, ys, yr, xs, xr, xl, rs, rr, rl, gys, gyr, gzs, gzr, outs,
):
    g = lax.axis_index("gz")
    h = lax.axis_index("gy")
    part = lax.rem(g, 2)
    other = 1 - part
    partner = g + 1 - 2 * part
    vectors, planes, rows, columns = block.shape
    mine = vectors // 2
    deep = 2 * planes
    low_z, high_z = g >= 2, g < nz - 2
    low_y, high_y = h >= 1, h < ny - 1

    def remote(src, dst, send, recv, gz, gy):
        return pltpu.make_async_remote_copy(
            src_ref=src, dst_ref=dst, send_sem=send, recv_sem=recv,
            device_id={"gz": gz, "gy": gy}, device_id_type=pl.DeviceIdType.MESH,
        )

    barrier = pltpu.get_barrier_semaphore()
    for d in range(1, nz):
        pl.semaphore_signal(barrier, inc=1, device_id={"gz": lax.rem(g + d, nz), "gy": h}, device_id_type=pl.DeviceIdType.MESH)
    for d in range(1, ny):
        pl.semaphore_signal(barrier, inc=1, device_id={"gz": g, "gy": lax.rem(h + d, ny)}, device_id_type=pl.DeviceIdType.MESH)

    zero_plane = jnp.zeros((rows, columns), jnp.float32)
    zero_rows = jnp.zeros((deep, columns), jnp.float32)

    @pl.when(jnp.logical_not(low_z))
    def _():
        coef[0] = zero_plane
        for v in range(mine):
            for slot in range(2):
                field[v, slot, 0] = zero_plane

    @pl.when(jnp.logical_not(high_z))
    def _():
        coef[deep + 1] = zero_plane
        for v in range(mine):
            for slot in range(2):
                field[v, slot, deep + 1] = zero_plane

    @pl.when(jnp.logical_not(low_y))
    def _():
        for v in range(mine + 1):
            for slot in range(2):
                yhalo[v, slot, 0] = zero_rows

    @pl.when(jnp.logical_not(high_y))
    def _():
        for v in range(mine + 1):
            for slot in range(2):
                yhalo[v, slot, 1] = zero_rows

    here = pl.ds(1 + planes * part, planes)
    there = pl.ds(1 + planes * other, planes)
    local_c = pltpu.make_async_copy(conduct, coef.at[here], xl.at[mine])
    local_v = [
        pltpu.make_async_copy(block.at[mine * part + v], field.at[v, 0, here], xl.at[v])
        for v in range(mine)
    ]
    swap_c = remote(conduct, coef.at[here], xs.at[mine], xr.at[mine], partner, h)
    swap_v = [
        remote(block.at[mine * other + v], field.at[v, 0, here], xs.at[v], xr.at[v], partner, h)
        for v in range(mine)
    ]
    local_c.start()
    for v in range(mine):
        local_v[v].start()
    pl.semaphore_wait(barrier, nz + ny - 2)
    swap_c.start()
    for v in range(mine):
        swap_v[v].start()

    def edges(body, v, slot):
        return [
            (low_z, remote(body.at[1], body.at[deep + 1], zs.at[v, slot, 0], zr.at[v, slot, 1], g - 2, h)),
            (high_z, remote(body.at[deep], body.at[0], zs.at[v, slot, 1], zr.at[v, slot, 0], g + 2, h)),
            (low_y, remote(ysend.at[v, slot, 0], yhalo.at[v, slot, 1], ys.at[v, slot, 0], yr.at[v, slot, 1], g, h - 1)),
            (high_y, remote(ysend.at[v, slot, 1], yhalo.at[v, slot, 0], ys.at[v, slot, 1], yr.at[v, slot, 0], g, h + 1)),
        ]

    def arrivals(body, v, slot):
        return [
            (high_z, remote(body.at[1], body.at[deep + 1], zs.at[v, slot, 0], zr.at[v, slot, 1], g + 2, h)),
            (low_z, remote(body.at[deep], body.at[0], zs.at[v, slot, 1], zr.at[v, slot, 0], g - 2, h)),
            (high_y, remote(ysend.at[v, slot, 0], yhalo.at[v, slot, 1], ys.at[v, slot, 0], yr.at[v, slot, 1], g, h + 1)),
            (low_y, remote(ysend.at[v, slot, 1], yhalo.at[v, slot, 0], ys.at[v, slot, 1], yr.at[v, slot, 0], g, h - 1)),
        ]

    def send_edges(body, v, slot):
        for cond, copy in edges(body, v, slot):
            pl.when(cond)(copy.start)

    def sent_edges(body, v, slot):
        for cond, copy in edges(body, v, slot):
            pl.when(cond)(copy.wait_send)

    def got_edges(body, v, slot):
        for cond, copy in arrivals(body, v, slot):
            pl.when(cond)(copy.wait_recv)

    def take_rows(body, v, slot):
        @pl.loop(0, deep)
        def _(z):
            ysend[v, slot, 0, pl.ds(z, 1), :] = body[z + 1, 0:1, :]
            ysend[v, slot, 1, pl.ds(z, 1), :] = body[z + 1, rows - 1 : rows, :]

    row_id = lax.broadcasted_iota(jnp.int32, (rows, columns), 0)
    col_id = lax.broadcasted_iota(jnp.int32, (rows, columns), 1)

    def y_neighbours(plane, v, slot, z):
        below = jnp.where(row_id == 0, yhalo[v, slot, 0, pl.ds(z, 1), :], pltpu.roll(plane, 1, 0))
        above = jnp.where(row_id == rows - 1, yhalo[v, slot, 1, pl.ds(z, 1), :], pltpu.roll(plane, rows - 1, 0))
        return below, above

    def x_neighbours(plane):
        return pltpu.roll(plane, 1, 1), pltpu.roll(plane, columns - 1, 1)

    local_c.wait()
    swap_c.wait_recv()
    take_rows(coef, mine, 0)
    send_edges(coef, mine, 0)
    got_edges(coef, mine, 0)
    scale = 1.0 / half_width
    wz[0] = scale * (coef[0] + coef[1])

    @pl.loop(0, deep)
    def _(z):
        plane = coef[z + 1]
        below, above = y_neighbours(plane, mine, 0, z)
        left, right = x_neighbours(plane)
        left = jnp.where(col_id == 0, 0.0, left)
        right = jnp.where(col_id == columns - 1, 0.0, right)
        zp = scale * (plane + coef[z + 2])
        zm = scale * (plane + coef[z])
        yp = scale * (plane + above)
        ym = scale * (plane + below)
        xp = scale * (plane + right)
        xm = scale * (plane + left)
        wz[z + 1] = zp
        wyp[z] = yp
        wym[z] = ym
        wxp[z] = jnp.where(col_id == columns - 1, 0.0, xp)
        wxm[z] = jnp.where(col_id == 0, 0.0, xm)
        diag[z] = (zp + zm) + (yp + ym) + (xp + xm) - (2.0 * mid_point / half_width)

    def advance(v, step):
        slot, later = step % 2, (step + 1) % 2
        now, nxt = field.at[v, slot], field.at[v, later]
        first = step % DEG == 0
        if step >= 1:
            sent_edges(nxt, v, later)
        got_edges(now, v, slot)

        @pl.loop(0, deep)
        def _(z):
            plane = now[z + 1]
            below, above = y_neighbours(plane, v, slot, z)
            left, right = x_neighbours(plane)
            total = diag[z] * plane
            total -= wz[z] * now[z] + wz[z + 1] * now[z + 2]
            total -= wym[z] * below + wyp[z] * above
            total -= wxm[z] * left + wxp[z] * right
            if first:
                total = 0.5 * total
            else:
                total = total - nxt[z + 1]
            nxt[z + 1] = total
            if step < STEPS - 1:
                ysend[v, later, 0, pl.ds(z, 1), :] = total[0:1, :]
                ysend[v, later, 1, pl.ds(z, 1), :] = total[rows - 1 : rows, :]

        if step < STEPS - 1:
            send_edges(nxt, v, later)

    def give_back(v):
        return remote(field.at[v, STEPS % 2, there], gathered.at[mine * part + v], rs.at[v], rr.at[v], partner, h)

    def keep(v):
        return pltpu.make_async_copy(field.at[v, STEPS % 2, here], gathered.at[mine * part + v], rl.at[v])

    for tick in range(STEPS + 1 + STRIDE * (mine - 1)):
        for v in range(mine):
            step = tick - STRIDE * v - 1
            if step == -1:
                local_v[v].wait()
                swap_v[v].wait_recv()
                take_rows(field.at[v, 0], v, 0)
                send_edges(field.at[v, 0], v, 0)
            elif 0 <= step < STEPS:
                advance(v, step)
                if step == STEPS - 1:
                    give_back(v).start()
                    keep(v).start()

    for v in range(mine):
        keep(v).wait()
        remote(field.at[v, STEPS % 2, there], gathered.at[mine * other + v], rs.at[v], rr.at[v], partner, h).wait_recv()
    to_out = pltpu.make_async_copy(gathered, filtered, outs)
    to_out.start()

    index = [(i, j) for i in range(vectors) for j in range(i + 1)]
    tiles = rows // 8

    def gram_body(t, accs):
        z, r = t // tiles, pl.multiple_of((t % tiles) * 8, 8)
        accs = list(accs)
        for c in range(columns // 128):
            vals = [gathered[v, z, pl.ds(r, 8), c * 128 : (c + 1) * 128] for v in range(vectors)]
            for p, (i, j) in enumerate(index):
                accs[p] = accs[p] + vals[i] * vals[j]
        return tuple(accs)

    accs = lax.fori_loop(0, planes * tiles, gram_body, tuple(jnp.zeros((8, 128), jnp.float32) for _ in index))
    pairs[...] = jnp.zeros((128, 128), jnp.float32)
    for p, (i, j) in enumerate(index):
        line = jnp.sum(accs[p], axis=0, keepdims=True)
        pairs[i * vectors + j : i * vectors + j + 1, :] = line
        if i != j:
            pairs[j * vectors + i : j * vectors + i + 1, :] = line
    ones = jnp.ones((8, 128), jnp.float32)
    part_sum = lax.dot_general(
        ones, pairs[...], (((1,), (1,)), ((), ())), precision=lax.Precision.HIGHEST,
        preferred_element_type=jnp.float32,
    )

    def total_of(value, slots, send, recv, axis, me, count):
        slots[me] = value
        copies = []
        for d in range(1, count):
            target = lax.rem(me + d, count)
            gz, gy = (target, h) if axis == "gz" else (g, target)
            copy = remote(slots.at[me], slots.at[me], send.at[d - 1], recv.at[d - 1], gz, gy)
            copy.start()
            copies.append(copy)
        for d in range(1, count):
            source = lax.rem(me - d + count, count)
            gz, gy = (source, h) if axis == "gz" else (g, source)
            remote(slots.at[source], slots.at[source], send.at[d - 1], recv.at[d - 1], gz, gy).wait_recv()
        result = slots[0]
        for d in range(1, count):
            result = result + slots[d]
        for copy in copies:
            copy.wait_send()
        return result

    slab = total_of(part_sum, gsum_y, gys, gyr, "gy", h, ny)
    gram_out[...] = total_of(slab, gsum_z, gzs, gzr, "gz", g, nz)

    swap_c.wait_send()
    sent_edges(coef, mine, 0)
    for v in range(mine):
        swap_v[v].wait_send()
        sent_edges(field.at[v, (STEPS - 1) % 2], v, (STEPS - 1) % 2)
        give_back(v).wait_send()
    to_out.wait()


def filter_and_gram(block, conduct):
    nz, ny = lax.axis_size("gz"), lax.axis_size("gy")
    vectors, planes, rows, columns = block.shape
    mine, deep = vectors // 2, 2 * planes
    f32 = jnp.float32
    dma = pltpu.SemaphoreType.DMA
    volume = pltpu.VMEM((deep, rows, columns), f32)
    return pl.pallas_call(
        functools.partial(kernel, nz, ny),
        out_shape=[jax.ShapeDtypeStruct(block.shape, f32), jax.ShapeDtypeStruct((8, 128), f32)],
        in_specs=[pl.BlockSpec(memory_space=pl.ANY)] * 2,
        out_specs=[pl.BlockSpec(memory_space=pl.ANY), pl.BlockSpec(memory_space=pltpu.VMEM)],
        scratch_shapes=[
            pltpu.VMEM((mine, 2, deep + 2, rows, columns), f32),
            pltpu.VMEM((deep + 2, rows, columns), f32),
            pltpu.VMEM((deep + 1, rows, columns), f32),
            volume, volume, volume, volume, volume,
            pltpu.VMEM((mine + 1, 2, 2, deep, columns), f32),
            pltpu.VMEM((mine + 1, 2, 2, deep, columns), f32),
            pltpu.VMEM((vectors, planes, rows, columns), f32),
            pltpu.VMEM((128, 128), f32),
            pltpu.VMEM((ny, 8, 128), f32),
            pltpu.VMEM((nz, 8, 128), f32),
            dma((mine + 1, 2, 2)), dma((mine + 1, 2, 2)), dma((mine + 1, 2, 2)), dma((mine + 1, 2, 2)),
            dma((mine + 1,)), dma((mine + 1,)), dma((mine + 1,)),
            dma((mine,)), dma((mine,)), dma((mine,)),
            dma((ny,)), dma((ny,)), dma((nz,)), dma((nz,)),
            dma,
        ],
        compiler_params=pltpu.CompilerParams(
            collective_id=0, has_side_effects=True, vmem_limit_bytes=40 * 1024 * 1024
        ),
        name="filter_and_gram",
    )(block, conduct)


def shards(block, conduct):
    vectors, planes, rows, columns = block.shape
    field, sums = filter_and_gram(block, conduct)
    gram = sums[0, : vectors * vectors].reshape(vectors, vectors)
    lower = jnp.linalg.cholesky(gram)
    inverse = lax.linalg.triangular_solve(
        lower, jnp.eye(vectors, dtype=jnp.float32), left_side=True, lower=True
    )
    total_cells = columns * rows * planes * lax.axis_size("gz") * lax.axis_size("gy")
    flat = field.reshape(vectors, -1)
    scaled = jnp.dot(inverse * math.sqrt(total_cells), flat, precision=lax.Precision.HIGHEST)
    return scaled.reshape(field.shape)


def solution(mesh):
    in_specs = (P(None, "gz", "gy", None), P("gz", "gy", None))
    out_specs = P(None, "gz", "gy", None)
    return jax.shard_map(shards, mesh=mesh, in_specs=in_specs, out_specs=out_specs, check_vma=False)
```

time: 286 us -> 114 us (0.40)
  Pallas kernels: 0 us -> 103 us
  starting transfers between devices: 95.9 us -> 0 us
  waiting for transfers between devices: 89.7 us -> 0 us
  other arithmetic: 54.4 us -> 2.68 us
  blocking collectives: 30.4 us -> 0 us
  matrix products: 6.63 us -> 2.07 us
    pallas_call x0 -> x1, Pallas kernels: none -> 103 us  [filter_and_gram(): pl.pallas_call(functools.partial(kernel, nz, ny), out_shape=[jax.ShapeDty...]
    ppermute x36 -> x0, starting transfers between devices: 95.9 us -> none  [the longest x18 72.2 us: with_halo(): lax.ppermute(lax.slice_in_dim(block, block.shape[dim] - width, None, axis...]
    ppermute x36 -> x0, waiting for transfers between devices: 89.7 us -> none  [the longest x18 64.7 us: with_halo(): lax.ppermute(lax.slice_in_dim(block, 0, width, axis=dim), axis, backward)]
    psum x2 -> x0, blocking collectives: 30.4 us -> none  [shards(): gram = lax.psum(lax.psum(local_gram, 'gy'), 'gz')]
    sub x6 -> x0, other arithmetic: 22.7 us -> none  [single_step(): return 2.0 * (image - mid_point * current) / half_width - previous]
    concatenate x16 -> x0, other arithmetic: 22.5 us -> none  [with_halo(): block = jnp.concatenate([low, block, high], axis=dim)]
    div x2 -> x0, other arithmetic: 6.3 us -> none  [single_step(): return (image - mid_point * current) / half_width]
    dot_general x2 -> x1, matrix products: 6.45 us -> 1.89 us  [shards(): jnp.dot(inverse * math.sqrt(total_cells), flat, precision=lax.Precision.H...]
  transfers between devices with their start and end apart: 36 -> 0, of which waited for: 24 -> 0; matrix products, arithmetic and copies ran while one was open for 2% -> 0% of each run, Pallas kernels for 0% -> 0%
where the time goes in v1:
time: 114 us; the launch traced here: 113 us
  Pallas kernels  103 us (90%)
  local copies, waits for them, and re-layouts  5.89 us (5%)
  other arithmetic  2.68 us (2%)
  matrix products  2.07 us (2%)
    pallas_call x1, Pallas kernels, filter_and_gram(): pl.pallas_call(functools.partial(kernel, nz, ny), out_shape=[jax.ShapeDty...  103 us
    unnamed x5, local copies, waits for them, and re-layouts  3.76 us

profile of v1, /device:TPU:0, one launch (start us, length us, event | category | flops | bytes accessed | tf_op | source)
XLA Modules:
  0.0 113.3 jit_solution(5943389422188518448)
XLA Ops:
  0.0 0.0 copy-start
  0.0 1.6 %copy-done = f32[8,8,32,256]{3,2,1,0:T(8,128)S(1)} copy-done((f32[8,8,32,256]{3,2,1,0:T(8,128)S(1)}, f32[8,8,32,256]{3,2,1,0:T(8,128)}, u32[]{:S(2)}) %copy-start) | copy-done | bytes 2097176
  1.6 0.0 copy-start.1
  1.6 0.9 copy-done.1
  2.5 102.7 %filter_and_gram.1 = (f32[8,8,32,256]{3,2,1,0:T(8,128)S(1)}, f32[8,128]{1,0:T(8,128)S(1)}) custom-call(f32[8,8,32,256]{3,2,1,0:T(8,128)S(1)} %copy-done, f32[8,32,256]{2,1,0:T(8,128)S(1)} %copy-done.1), custom_call_target="tpu_custom_call" | custom-call | tf_op jit(solution)/shard_map/filter_and_gram/pallas_call | solution.py:291
  105.2 1.2 %copy.7 = f32[1,8,256,256]{3,1,2,0:T(8,128)S(1)} copy(f32[1,8,256,256]{3,2,1,0:T(8,128)S(1)} %bitcast.23) | data formatting | bytes 4194304
  106.4 0.1 reshape_squeeze.3
  106.5 0.1 copy.3
  106.6 0.7 cholesky.17
  107.3 0.1 select_reduce_fusion
  107.4 0.6 compare_reduce_fusion
  108.0 0.6 fusion.1
  108.7 0.6 custom-call.6
  109.3 0.2 fusion
  109.5 1.9 %fusion.4 = f32[8,8,32,256]{3,0,2,1:T(8,128)S(1)} fusion(f32[8,8,1,1]{1,0,3,2:T(8,128)S(1)} %fusion, f32[8,32,256,8]{2,3,1,0:T(8,128)S(1)} %bitcast.24), kind=kOutput, calls=%fused_computation.12 | convolution fusion | flops 50331648 | bytes 4194560 | tf_op jit(solution)/shard_map/dot_general | solution.py:330
  111.4 2.0 %copy.5 = f32[8,8,32,256]{3,2,1,0:T(8,128)} copy(f32[8,8,32,256]{3,0,2,1:T(8,128)S(1)} %fusion.4) | data formatting | bytes 4194304 | tf_op jit(solution)/shard_map/dot_general | solution.py:330
  (2 shorter events, 0.0 us)
Async XLA Ops:
  0.0 1.6 %copy-start = (f32[8,8,32,256]{3,2,1,0:T(8,128)S(1)}, f32[8,8,32,256]{3,2,1,0:T(8,128)}, u32[]{:S(2)}) copy-start(f32[8,8,32,256]{3,2,1,0:T(8,128)} %block.1) | copy-start | bytes 6291460
  1.6 0.9 copy-start.1

commit v2 on v1

--- a/solution.py
+++ b/solution.py
@@ -11,10 +11,25 @@
 DEG = 4
 PASSES = 2
 STEPS = DEG * PASSES
-STRIDE = 2
+UNROLL = 7
+MODEL = (14.0, 5.7, 2.3, 0.5)
 
 mid_point = 12.75
 half_width = 11.25
+
+
+def task_order(count):
+    first, apart, trip, work = MODEL
+    ready = [first + apart * v for v in range(count)]
+    step = [-1] * count
+    now, order = 0.0, []
+    while min(step) < STEPS:
+        v = min((u for u in range(count) if step[u] < STEPS), key=lambda u: (max(ready[u], now), ready[u], u))
+        now = max(now, ready[v]) + (work if step[v] >= 0 else 0.1)
+        ready[v] = now + trip
+        order.append((v, step[v]))
+        step[v] += 1
+    return order
 
 
 def kernel(
@@ -112,8 +127,12 @@
             (low_y, remote(ysend.at[v, slot, 1], yhalo.at[v, slot, 0], ys.at[v, slot, 1], yr.at[v, slot, 0], g, h - 1)),
         ]
 
-    def send_edges(body, v, slot):
-        for cond, copy in edges(body, v, slot):
+    def send_z(body, v, slot):
+        for cond, copy in edges(body, v, slot)[:2]:
+            pl.when(cond)(copy.start)
+
+    def send_y(body, v, slot):
+        for cond, copy in edges(body, v, slot)[2:]:
             pl.when(cond)(copy.start)
 
     def sent_edges(body, v, slot):
@@ -143,8 +162,9 @@
 
     local_c.wait()
     swap_c.wait_recv()
+    send_z(coef, mine, 0)
     take_rows(coef, mine, 0)
-    send_edges(coef, mine, 0)
+    send_y(coef, mine, 0)
     got_edges(coef, mine, 0)
     scale = 1.0 / half_width
     wz[0] = scale * (coef[0] + coef[1])
@@ -177,8 +197,7 @@
             sent_edges(nxt, v, later)
         got_edges(now, v, slot)
 
-        @pl.loop(0, deep)
-        def _(z):
+        def one_plane(z):
             plane = now[z + 1]
             below, above = y_neighbours(plane, v, slot, z)
             left, right = x_neighbours(plane)
@@ -195,8 +214,13 @@
                 ysend[v, later, 0, pl.ds(z, 1), :] = total[0:1, :]
                 ysend[v, later, 1, pl.ds(z, 1), :] = total[rows - 1 : rows, :]
 
+        one_plane(0)
+        one_plane(deep - 1)
         if step < STEPS - 1:
-            send_edges(nxt, v, later)
+            send_z(nxt, v, later)
+        pl.loop(1, deep - 1, unroll=UNROLL)(one_plane)
+        if step < STEPS - 1:
+            send_y(nxt, v, later)
 
     def give_back(v):
         return remote(field.at[v, STEPS % 2, there], gathered.at[mine * part + v], rs.at[v], rr.at[v], partner, h)
@@ -204,19 +228,18 @@
     def keep(v):
         return pltpu.make_async_copy(field.at[v, STEPS % 2, here], gathered.at[mine * part + v], rl.at[v])
 
-    for tick in range(STEPS + 1 + STRIDE * (mine - 1)):
-        for v in range(mine):
-            step = tick - STRIDE * v - 1
-            if step == -1:
-                local_v[v].wait()
-                swap_v[v].wait_recv()
-                take_rows(field.at[v, 0], v, 0)
-                send_edges(field.at[v, 0], v, 0)
-            elif 0 <= step < STEPS:
-                advance(v, step)
-                if step == STEPS - 1:
-                    give_back(v).start()
-                    keep(v).start()
+    for v, step in task_order(mine):
+        if step < 0:
+            local_v[v].wait()
+            swap_v[v].wait_recv()
+            send_z(field.at[v, 0], v, 0)
+            take_rows(field.at[v, 0], v, 0)
+            send_y(field.at[v, 0], v, 0)
+        else:
+            advance(v, step)
+            if step == STEPS - 1:
+                give_back(v).start()
+                keep(v).start()
 
     for v in range(mine):
         keep(v).wait()
@@ -311,24 +334,67 @@
             dma,
         ],
         compiler_params=pltpu.CompilerParams(
-            collective_id=0, has_side_effects=True, vmem_limit_bytes=40 * 1024 * 1024
+            collective_id=0, has_side_effects=True, vmem_limit_bytes=60 * 1024 * 1024
         ),
         name="filter_and_gram",
     )(block, conduct)
 
 
+def finish_kernel(cells, sums, field, basis, inverse):
+    vectors = field.shape[0]
+
+    @pl.when(pl.program_id(0) == 0)
+    def _():
+        gram = sums[...]
+        low = {}
+        recip = []
+        for j in range(vectors):
+            for i in range(j, vectors):
+                at = i * vectors + j
+                value = jnp.broadcast_to(gram[:, at : at + 1], (8, 128))
+                for k in range(j):
+                    value = value - low[i, k] * low[j, k]
+                if i == j:
+                    low[j, j] = jnp.sqrt(value)
+                    recip.append(1.0 / low[j, j])
+                else:
+                    low[i, j] = value * recip[j]
+        for j in range(vectors):
+            column = {j: recip[j]}
+            for i in range(j + 1, vectors):
+                value = low[i, j] * column[j]
+                for k in range(j + 1, i):
+                    value = value + low[i, k] * column[k]
+                column[i] = -value * recip[i]
+            for i in range(j, vectors):
+                inverse[i * vectors + j] = column[i] * math.sqrt(cells)
+
+    factors = {(i, j): inverse[i * vectors + j] for i in range(vectors) for j in range(i + 1)}
+    rows, columns = field.shape[2:]
+    for r in range(0, rows, 8):
+        for c in range(0, columns, 128):
+            vals = [field[v, 0, r : r + 8, c : c + 128] for v in range(vectors)]
+            for i in range(vectors):
+                total = factors[i, 0] * vals[0]
+                for j in range(1, i + 1):
+                    total = total + factors[i, j] * vals[j]
+                basis[i, 0, r : r + 8, c : c + 128] = total
+
+
 def shards(block, conduct):
     vectors, planes, rows, columns = block.shape
     field, sums = filter_and_gram(block, conduct)
-    gram = sums[0, : vectors * vectors].reshape(vectors, vectors)
-    lower = jnp.linalg.cholesky(gram)
-    inverse = lax.linalg.triangular_solve(
-        lower, jnp.eye(vectors, dtype=jnp.float32), left_side=True, lower=True
-    )
     total_cells = columns * rows * planes * lax.axis_size("gz") * lax.axis_size("gy")
-    flat = field.reshape(vectors, -1)
-    scaled = jnp.dot(inverse * math.sqrt(total_cells), flat, precision=lax.Precision.HIGHEST)
-    return scaled.reshape(field.shape)
+    spec = pl.BlockSpec((vectors, 1, rows, columns), lambda z: (0, z, 0, 0))
+    return pl.pallas_call(
+        functools.partial(finish_kernel, total_cells),
+        grid=(planes,),
+        out_shape=jax.ShapeDtypeStruct(block.shape, jnp.float32),
+        in_specs=[pl.BlockSpec((8, 128), lambda z: (0, 0)), spec],
+        out_specs=spec,
+        scratch_shapes=[pltpu.VMEM((vectors * vectors, 8, 128), jnp.float32)],
+        name="finish",
+    )(sums, field)
 
 
 def solution(mesh):

time: 114 us -> 87.1 us (0.76)
  Pallas kernels: 103 us -> 86.8 us
  local copies, waits for them, and re-layouts: 5.89 us -> 0 us
  other arithmetic: 2.68 us -> 0 us
  matrix products: 2.07 us -> 0 us
    pallas_call x1, Pallas kernels: 103 us -> 80.8 us  [filter_and_gram(): pl.pallas_call(functools.partial(kernel, nz, ny), out_shape=[jax.ShapeDty...]
    pallas_call x0 -> x1, Pallas kernels: none -> 6.1 us  [shards(): pl.pallas_call(functools.partial(finish_kernel, total_cells), grid=(plane...]
    unnamed x5 -> x0, local copies, waits for them, and re-layouts: 3.76 us -> none
    another operation x5 -> x0, other arithmetic: 2.67 us -> none  [the longest x3 1.4 us: shards(): lower = jnp.linalg.cholesky(gram)]
    dot_general x1 -> x0, local copies, waits for them, and re-layouts: 1.96 us -> none  [shards(): jnp.dot(inverse * math.sqrt(total_cells), flat, precision=lax.Precision.H...]
    dot_general x1 -> x0, matrix products: 1.89 us -> none  [shards(): jnp.dot(inverse * math.sqrt(total_cells), flat, precision=lax.Precision.H...]
where the time goes in v2:
time: 87.1 us; the launch traced here: 86.9 us
  Pallas kernels  86.8 us (100%)
    pallas_call x1, Pallas kernels, filter_and_gram(): pl.pallas_call(functools.partial(kernel, nz, ny), out_shape=[jax.ShapeDty...  80.8 us
    pallas_call x1, Pallas kernels, shards(): pl.pallas_call(functools.partial(finish_kernel, total_cells), grid=(plane...  6.1 us

profile of v2, /device:TPU:0, one launch (start us, length us, event | category | flops | bytes accessed | tf_op | source)
XLA Modules:
  0.0 86.9 jit_solution(3808643527720064866)
XLA Ops:
  0.0 80.8 %filter_and_gram.1 = (f32[8,8,32,256]{3,2,1,0:T(8,128)}, f32[8,128]{1,0:T(8,128)}) custom-call(f32[8,8,32,256]{3,2,1,0:T(8,128)} %block.1, f32[8,32,256]{2,1,0:T(8,128)} %conduct.1), custom_call_target="tpu_custom_call" | custom-call | tf_op jit(solution)/shard_map/filter_and_gram/pallas_call | solution.py:314
  80.8 6.1 %finish.1 = f32[8,8,32,256]{3,2,1,0:T(8,128)} custom-call(f32[8,128]{1,0:T(8,128)} %get-tuple-element.7.sums, f32[8,8,32,256]{3,2,1,0:T(8,128)} %get-tuple-element.8.field), custom_call_target="tpu_custom_call" | custom-call | tf_op jit(solution)/shard_map/finish/pallas_call | solution.py:389

commit v3 on v2

--- a/solution.py
+++ b/solution.py
@@ -12,7 +12,7 @@
 PASSES = 2
 STEPS = DEG * PASSES
 UNROLL = 7
-MODEL = (14.0, 5.7, 2.3, 0.5)
+MODEL = (14.0, 5.7, 2.8, 0.6)
 
 mid_point = 12.75
 half_width = 11.25
@@ -37,7 +37,8 @@
     block, conduct, filtered, gram_out,
     field, coef, wz, wym, wyp, wxm, wxp, diag,
     yhalo, ysend, gathered, pairs, gsum_y, gsum_z,
-    zs, zr, ys, yr, xs, xr, xl, rs, rr, rl, gys, gyr, gzs, gzr, outs,
+    outbox, outbox_c,
+    bl, zs, zr, ys, yr, xs, xr, xl, rs, rr, rl, gys, gyr, gzs, gzr, outs,
 ):
     g = lax.axis_index("gz")
     h = lax.axis_index("gy")
@@ -98,17 +99,27 @@
         pltpu.make_async_copy(block.at[mine * part + v], field.at[v, 0, here], xl.at[v])
         for v in range(mine)
     ]
-    swap_c = remote(conduct, coef.at[here], xs.at[mine], xr.at[mine], partner, h)
-    swap_v = [
-        remote(block.at[mine * other + v], field.at[v, 0, here], xs.at[v], xr.at[v], partner, h)
+    load_c = pltpu.make_async_copy(conduct, outbox_c, bl.at[mine])
+    load_v = [
+        pltpu.make_async_copy(block.at[mine * other + v], outbox.at[v], bl.at[v])
         for v in range(mine)
     ]
+    swap_c = remote(outbox_c, coef.at[here], xs.at[mine], xr.at[mine], partner, h)
+    swap_v = [
+        remote(outbox.at[v], field.at[v, 0, here], xs.at[v], xr.at[v], partner, h)
+        for v in range(mine)
+    ]
+    load_c.start()
+    for v in range(mine):
+        load_v[v].start()
     local_c.start()
     for v in range(mine):
         local_v[v].start()
     pl.semaphore_wait(barrier, nz + ny - 2)
+    load_c.wait()
     swap_c.start()
     for v in range(mine):
+        load_v[v].wait()
         swap_v[v].start()
 
     def edges(body, v, slot):
@@ -327,6 +338,9 @@
             pltpu.VMEM((128, 128), f32),
             pltpu.VMEM((ny, 8, 128), f32),
             pltpu.VMEM((nz, 8, 128), f32),
+            pltpu.VMEM((mine, planes, rows, columns), f32),
+            pltpu.VMEM((planes, rows, columns), f32),
+            dma((mine + 1,)),
             dma((mine + 1, 2, 2)), dma((mine + 1, 2, 2)), dma((mine + 1, 2, 2)), dma((mine + 1, 2, 2)),
             dma((mine + 1,)), dma((mine + 1,)), dma((mine + 1,)),
             dma((mine,)), dma((mine,)), dma((mine,)),
@@ -340,59 +354,68 @@
     )(block, conduct)
 
 
-def finish_kernel(cells, sums, field, basis, inverse):
-    vectors = field.shape[0]
-
-    @pl.when(pl.program_id(0) == 0)
-    def _():
-        gram = sums[...]
-        low = {}
-        recip = []
-        for j in range(vectors):
-            for i in range(j, vectors):
-                at = i * vectors + j
-                value = jnp.broadcast_to(gram[:, at : at + 1], (8, 128))
-                for k in range(j):
-                    value = value - low[i, k] * low[j, k]
-                if i == j:
-                    low[j, j] = jnp.sqrt(value)
-                    recip.append(1.0 / low[j, j])
-                else:
-                    low[i, j] = value * recip[j]
-        for j in range(vectors):
-            column = {j: recip[j]}
-            for i in range(j + 1, vectors):
-                value = low[i, j] * column[j]
-                for k in range(j + 1, i):
-                    value = value + low[i, k] * column[k]
-                column[i] = -value * recip[i]
-            for i in range(j, vectors):
-                inverse[i * vectors + j] = column[i] * math.sqrt(cells)
-
-    factors = {(i, j): inverse[i * vectors + j] for i in range(vectors) for j in range(i + 1)}
-    rows, columns = field.shape[2:]
-    for r in range(0, rows, 8):
-        for c in range(0, columns, 128):
-            vals = [field[v, 0, r : r + 8, c : c + 128] for v in range(vectors)]
-            for i in range(vectors):
-                total = factors[i, 0] * vals[0]
-                for j in range(1, i + 1):
-                    total = total + factors[i, j] * vals[j]
-                basis[i, 0, r : r + 8, c : c + 128] = total
+def finish_kernel(cells, sums, field, basis, held, result, taken, given):
+    vectors, planes, rows, columns = field.shape
+    take = [pltpu.make_async_copy(field.at[:, z], held.at[:, z], taken.at[z]) for z in range(planes)]
+    give = [pltpu.make_async_copy(result.at[:, z], basis.at[:, z], given.at[z]) for z in range(planes)]
+    for z in range(planes):
+        take[z].start()
+    gram = sums[...]
+    low = {}
+    factors = {}
+    recip = []
+    for j in range(vectors):
+        for i in range(j, vectors):
+            at = i * vectors + j
+            value = jnp.broadcast_to(gram[:, at : at + 1], (8, 128))
+            for k in range(j):
+                value = value - low[i, k] * low[j, k]
+            if i == j:
+                low[j, j] = jnp.sqrt(value)
+                recip.append(1.0 / low[j, j])
+            else:
+                low[i, j] = value * recip[j]
+    for j in range(vectors):
+        column = {j: recip[j]}
+        for i in range(j + 1, vectors):
+            value = low[i, j] * column[j]
+            for k in range(j + 1, i):
+                value = value + low[i, k] * column[k]
+            column[i] = -value * recip[i]
+        for i in range(j, vectors):
+            factors[i, j] = column[i] * math.sqrt(cells)
+
+    for z in range(planes):
+        take[z].wait()
+
+        @pl.loop(0, rows, step=8)
+        def _(r):
+            r = pl.multiple_of(r, 8)
+            for c in range(0, columns, 128):
+                vals = [held[v, z, pl.ds(r, 8), c : c + 128] for v in range(vectors)]
+                for i in range(vectors):
+                    total = factors[i, 0] * vals[0]
+                    for j in range(1, i + 1):
+                        total = total + factors[i, j] * vals[j]
+                    result[i, z, pl.ds(r, 8), c : c + 128] = total
+
+        give[z].start()
+    for z in range(planes):
+        give[z].wait()
 
 
 def shards(block, conduct):
     vectors, planes, rows, columns = block.shape
     field, sums = filter_and_gram(block, conduct)
     total_cells = columns * rows * planes * lax.axis_size("gz") * lax.axis_size("gy")
-    spec = pl.BlockSpec((vectors, 1, rows, columns), lambda z: (0, z, 0, 0))
+    whole = pltpu.VMEM(block.shape, jnp.float32)
     return pl.pallas_call(
         functools.partial(finish_kernel, total_cells),
-        grid=(planes,),
         out_shape=jax.ShapeDtypeStruct(block.shape, jnp.float32),
-        in_specs=[pl.BlockSpec((8, 128), lambda z: (0, 0)), spec],
-        out_specs=spec,
-        scratch_shapes=[pltpu.VMEM((vectors * vectors, 8, 128), jnp.float32)],
+        in_specs=[pl.BlockSpec(memory_space=pltpu.VMEM), pl.BlockSpec(memory_space=pl.ANY)],
+        out_specs=pl.BlockSpec(memory_space=pl.ANY),
+        scratch_shapes=[whole, whole, pltpu.SemaphoreType.DMA((planes,)), pltpu.SemaphoreType.DMA((planes,))],
+        compiler_params=pltpu.CompilerParams(vmem_limit_bytes=60 * 1024 * 1024),
         name="finish",
     )(sums, field)
 

time: 87.1 us -> 82.3 us (0.945)
  Pallas kernels: 86.8 us -> 82.1 us
    pallas_call x1, Pallas kernels: 6.1 us -> 3.52 us  [shards(): pl.pallas_call(functools.partial(finish_kernel, total_cells), out_shape=j...]
    pallas_call x1, Pallas kernels: 80.8 us -> 78.6 us  [filter_and_gram(): pl.pallas_call(functools.partial(kernel, nz, ny), out_shape=[jax.ShapeDty...]
where the time goes in v3:
time: 82.3 us; the launch traced here: 82.1 us
  Pallas kernels  82.1 us (100%)
    pallas_call x1, Pallas kernels, filter_and_gram(): pl.pallas_call(functools.partial(kernel, nz, ny), out_shape=[jax.ShapeDty...  78.6 us
    pallas_call x1, Pallas kernels, shards(): pl.pallas_call(functools.partial(finish_kernel, total_cells), out_shape=j...  3.52 us

profile of v3, /device:TPU:0, one launch (start us, length us, event | category | flops | bytes accessed | tf_op | source)
XLA Modules:
  0.0 82.1 jit_solution(15809590096604304120)
XLA Ops:
  0.0 78.6 %filter_and_gram.1 = (f32[8,8,32,256]{3,2,1,0:T(8,128)}, f32[8,128]{1,0:T(8,128)}) custom-call(f32[8,8,32,256]{3,2,1,0:T(8,128)} %block.1, f32[8,32,256]{2,1,0:T(8,128)} %conduct.1), custom_call_target="tpu_custom_call" | custom-call | tf_op jit(solution)/shard_map/filter_and_gram/pallas_call | solution.py:325
  78.6 3.5 %finish.1 = f32[8,8,32,256]{3,2,1,0:T(8,128)} custom-call(f32[8,128]{1,0:T(8,128)} %get-tuple-element.7.sums, f32[8,8,32,256]{3,2,1,0:T(8,128)} %get-tuple-element.8.field), custom_call_target="tpu_custom_call" | custom-call | tf_op jit(solution)/shard_map/finish/pallas_call | solution.py:412
